TPU v7x, 256 devices: a whole 4x4x8 slice. The times are simulated.
256 devices in a mesh: pw: 64 (over x_lo, z, y), band: 4 (over x_hi, core).
Axes of the slice: x: 4 (x_hi: 2, x_lo: 2; x = x_hi * 2 + x_lo), y: 4, z: 8, core: 2. Of those that a mesh axis runs over, the one named last changes fastest.
Arguments:
- residual_directions: float32 [2, 512, 4, 16384], P(None, 'pw', 'band'), may hold values from -6 to 6
- local_field_applied: float32 [2, 512, 4, 16384], P(None, 'pw', 'band'), may hold values from -6 to 6
- orbital_running_sum: bfloat16 [2, 2048, 4, 16384], P(None, None, 'band', 'pw'), may hold values from -6 to 6
- energy_operator_running_sum: bfloat16 [2, 2048, 4, 16384], P(None, None, 'band', 'pw'), may hold values from -6 to 6
- coefficient_store: bfloat16 [4, 512, 2048], P('band'), may hold values from -0.25 to 0.25
- slab_keepers: int32 [2], replicated, may hold values from 0 to 3
- lattice_position: int32 [4, 16384], P('band', 'pw'), may hold values from 0 to 262143
Outputs:
- psi_new: bfloat16 [2, 2048, 4, 16384], P(None, None, 'band', 'pw')
- hpsi_new: bfloat16 [2, 2048, 4, 16384], P(None, None, 'band', 'pw')
Inputs may be any that keep to these rules, and one draw needn't show every extreme that they name: `slab_keepers`: each panel's owner is an index along band. `lattice_position`: grid points are row-major indices of a 64 x 64 x 64 grid, not necessarily distinct.
All inputs are finite; a program needn't handle non-finite values.
Results may differ from a plain program's by a relative error of at most 0.001.
Values may be sent and summed in bfloat16 or wider, within the bound.
No kernel may reach another device: no remote copies, remote signals or barrier semaphores. Data moves between devices by JAX's collectives and lax.ppermute only.
A program may use at most 128 MiB of HBM per device.

v0:
```python
import jax
import jax.numpy as jnp
from jax import lax
from jax.sharding import PartitionSpec as P

RESIDUAL_NUMBER = 512
SLAB_LENGTH = 256
GRID = 64


def from_root(value, axis, source):
    kept = jnp.where(lax.axis_index(axis) == source, value, 0).astype(value.dtype)
    return lax.psum(kept, axis)


def kinetic_of(lattice_position):
    first = lattice_position // (GRID * GRID)
    second = lattice_position // GRID % GRID
    third = lattice_position % GRID
    total = jnp.zeros(lattice_position.shape, jnp.int32)
    for index in (first, second, third):
        folded = jnp.where(index >= GRID // 2, index - GRID, index)
        total = total + folded * folded
    return total.astype(jnp.float32) / (GRID * GRID)


def rotate_plane(panels, plane):
    total = None
    for subspace_slab in range(len(panels)):
        block = plane[subspace_slab * SLAB_LENGTH : (subspace_slab + 1) * SLAB_LENGTH]
        term = lax.dot_general(
            panels[subspace_slab],
            block,
            (((0,), (0,)), ((), ())),
            precision=lax.Precision.HIGHEST,
            preferred_element_type=jnp.float32,
        )
        total = term if total is None else total + term
    return total


def per_device(
    residual_directions,
    local_field_applied,
    orbital_running_sum,
    energy_operator_running_sum,
    coefficient_store,
    slab_keepers,
    lattice_position,
):
    count = RESIDUAL_NUMBER // SLAB_LENGTH
    panels = []
    for subspace_slab in range(count):
        slab_piece = coefficient_store[
            0, subspace_slab * SLAB_LENGTH : (subspace_slab + 1) * SLAB_LENGTH
        ]
        panels.append(
            from_root(slab_piece, "band", slab_keepers[subspace_slab]).astype(jnp.float32)
        )
    outgoing = (residual_directions, local_field_applied)
    local_kinetic = kinetic_of(lattice_position)
    corr_part = lax.all_to_all(outgoing[0], "pw", split_axis=3, concat_axis=1, tiled=True)
    second_part = lax.all_to_all(outgoing[1], "pw", split_axis=3, concat_axis=1, tiled=True)
    planes_count = corr_part.shape[0]
    rows = corr_part.shape[1]
    width = corr_part.shape[3]
    corr_flat = corr_part.reshape(planes_count, rows, width)
    second_flat = second_part.reshape(planes_count, rows, width)
    hcorr_flat = local_kinetic.reshape(1, 1, width) * corr_flat + second_flat
    psi_planes = [
        rotate_plane(panels, corr_flat[plane_index]) for plane_index in range(planes_count)
    ]
    hpsi_planes = [
        rotate_plane(panels, hcorr_flat[plane_index]) for plane_index in range(planes_count)
    ]
    span = psi_planes[0].shape[0]
    psi_stack = jnp.stack(psi_planes, axis=0).reshape(planes_count, span, 1, width)
    hpsi_stack = jnp.stack(hpsi_planes, axis=0).reshape(planes_count, span, 1, width)
    psi_new = (orbital_running_sum.astype(jnp.float32) + psi_stack).astype(jnp.bfloat16)
    hpsi_new = (energy_operator_running_sum.astype(jnp.float32) + hpsi_stack).astype(jnp.bfloat16)
    return (psi_new, hpsi_new)


def solution(mesh):
    in_specs = (
        P(None, "pw", "band", None),
        P(None, "pw", "band", None),
        P(None, None, "band", "pw"),
        P(None, None, "band", "pw"),
        P("band", None, None),
        P(),
        P("band", "pw"),
    )
    out_specs = (P(None, None, "band", "pw"), P(None, None, "band", "pw"))
    return jax.shard_map(
        per_device, mesh=mesh, in_specs=in_specs, out_specs=out_specs, check_vma=False
    )
```

profile of v0, /device:TPU:1, one launch (start us, length us, event | category | flops | bytes accessed | tf_op | source)
XLA Modules:
  0.0 261.6 jit_solution(14496637142903261948)
XLA Ops:
  7.2 17.4 %copy.42 = f32[2,8,1,16384]{1,0,2,3:T(2,128)} copy(f32[2,8,1,16384]{3,2,1,0:T(1,128)} %param.7) | data formatting | bytes 2097152 | tf_op args[0]
  24.6 29.0 %reshape.42 = f32[64,1,4096]{2,1,0:T(1,128)} reshape(f32[16384,1,2,8]{3,2,1,0:T(2,128)} %bitcast.92) | data formatting | bytes 2097152
  53.5 13.7 %all-to-all-start = ((f32[64,1,4096]{2,1,0:T(1,128)}), f32[64,1,4096]{2,1,0:T(1,128)S(1)}, u32[]{:S(2)}, u32[]{:S(2)}) async-start(f32[64,1,4096]{2,1,0:T(1,128)} %reshape.42), calls=%async_computation | async-start | bytes 2097152 | tf_op jit(solution)/shard_map/all_to_all | solution.py:62
  67.2 14.6 %copy.50 = f32[2,8,1,16384]{1,0,2,3:T(2,128)} copy(f32[2,8,1,16384]{3,2,1,0:T(1,128)S(1)} %copy-done.4) | data formatting | bytes 2097152 | tf_op args[1]
  81.8 28.9 %reshape.44 = f32[64,1,4096]{2,1,0:T(1,128)} reshape(f32[16384,1,2,8]{3,2,1,0:T(2,128)} %bitcast.93) | data formatting | bytes 2097152
  110.8 11.1 %all-to-all-start.1 = ((f32[64,1,4096]{2,1,0:T(1,128)}), f32[64,1,4096]{2,1,0:T(1,128)}, u32[]{:S(2)}, u32[]{:S(2)}) async-start(f32[64,1,4096]{2,1,0:T(1,128)} %reshape.44), calls=%async_computation.1 | async-start | bytes 2097152 | tf_op jit(solution)/shard_map/all_to_all | solution.py:63
  124.0 3.0 %select_bitcast_fusion = (bf16[256,2048]{1,0:T(8,128)(2,1)}, bf16[256,2048]{1,0:T(8,128)(2,1)}) fusion(bf16[1,512,2048]{2,1,0:T(8,128)(2,1)} %param.11, pred[]{:T(512)S(6)} %eq.10, pred[]{:T(512)S(6)} %eq.9), kind=kLoop, calls=%fused_computation.18 | loop fusion | flops 1048576 | bytes 4194306 | tf_op jit(solution)/shard_map/jit(_where)/select_n | solution.py:12
  128.3 3.3 %reduce.1 = f32[64,4096]{1,0:T(8,128)S(1)} reduce(f32[64,1,4096]{2,1,0:T(1,128)S(1)} %all-to-all-done, f32[]{:T(128)} %broadcast.42), dimensions={1}, to_apply=%all_to_all.22.reduce_sub_computation | reduce | bytes 2097156 | tf_op jit(solution)/shard_map/all_to_all | solution.py:62
  131.6 26.7 %reshape.43 = f32[16384,1,2,8]{3,2,1,0:T(2,128)} reshape(f32[64,4096]{1,0:T(8,128)S(1)} %reduce.1) | data formatting | bytes 2097152
  158.3 17.7 %copy.56 = f32[2,8,1,64,256]{4,1,3,0,2:T(8,128)S(1)} copy(f32[2,8,1,64,256]{1,0,4,3,2:T(2,128)} %bitcast.89) | data formatting | bytes 2097152 | tf_op jit(solution)/shard_map/all_to_all | solution.py:62
  176.0 13.3 %copy.55 = f32[2,8,1,64,256]{4,3,1,0,2:T(8,128)S(1)} copy(f32[2,8,1,64,256]{1,0,4,3,2:T(2,128)} %bitcast.90) | data formatting | bytes 2097152 | tf_op jit(solution)/shard_map/all_to_all | solution.py:62
  189.3 4.4 %reduce = f32[64,4096]{1,0:T(8,128)S(1)} reduce(f32[64,1,4096]{2,1,0:T(1,128)} %all-to-all-done.1, f32[]{:T(128)} %broadcast.42), dimensions={1}, to_apply=%all_to_all.25.reduce_sub_computation | reduce | bytes 2097156 | tf_op jit(solution)/shard_map/all_to_all | solution.py:63
  193.7 26.7 %reshape.45 = f32[16384,1,2,8]{3,2,1,0:T(2,128)} reshape(f32[64,4096]{1,0:T(8,128)S(1)} %reduce) | data formatting | bytes 2097152
  220.4 17.8 %copy.58 = f32[2,8,1,64,256]{4,1,3,0,2:T(8,128)S(1)} copy(f32[2,8,1,64,256]{1,0,4,3,2:T(2,128)} %bitcast.91) | data formatting | bytes 2097152 | tf_op jit(solution)/shard_map/all_to_all | solution.py:63
  238.2 0.9 fusion.28
  239.3 2.6 fusion.10
  241.9 1.3 fusion.11
  243.2 1.3 fusion.4
  244.5 1.3 fusion.5
  245.9 1.3 fusion.13
  247.2 1.3 fusion.16
  248.6 1.4 fusion.6
  250.0 1.4 fusion.7
  252.2 2.5 fusion.8
  (29 shorter events, 3.1 us)
Async XLA Ops:
  53.5 13.7 %copy-start.4 = (f32[2,8,1,16384]{3,2,1,0:T(1,128)S(1)}, f32[2,8,1,16384]{3,2,1,0:T(1,128)}, u32[]{:S(2)}) copy-start(f32[2,8,1,16384]{3,2,1,0:T(1,128)} %param.8) | copy-start | bytes 3145732
  53.5 57.3 %all-to-all-start = ((f32[64,1,4096]{2,1,0:T(1,128)}), f32[64,1,4096]{2,1,0:T(1,128)S(1)}, u32[]{:S(2)}, u32[]{:S(2)}) async-start(f32[64,1,4096]{2,1,0:T(1,128)} %reshape.42), calls=%async_computation | async-start | bytes 2097152 | tf_op jit(solution)/shard_map/all_to_all | solution.py:62
  110.8 11.4 %copy-start.8 = (s32[2]{0:T(128)S(1)}, s32[2]{0:T(128)}, u32[]{:S(2)}) copy-start(s32[2]{0:T(128)} %param.12) | copy-start | bytes 28
  110.8 78.5 %all-to-all-start.1 = ((f32[64,1,4096]{2,1,0:T(1,128)}), f32[64,1,4096]{2,1,0:T(1,128)}, u32[]{:S(2)}, u32[]{:S(2)}) async-start(f32[64,1,4096]{2,1,0:T(1,128)} %reshape.44), calls=%async_computation.1 | async-start | bytes 2097152 | tf_op jit(solution)/shard_map/all_to_all | solution.py:63
  121.9 117.4 %all-reduce.3.cloned.1.call-start = ((), (), s32[]{:S(2)}) async-start(), calls=%async_computation.2 | async-start | bytes 4194304 | tf_op jit(solution)/shard_map/psum | solution.py:13
  127.0 0.7 copy-start.9
  239.3 2.6 copy-start
  241.9 1.3 copy-start.1
  244.5 1.3 copy-start.5
  247.2 1.4 copy-start.7
  248.6 1.4 copy-start.6
  250.0 1.6 copy-start.2
  250.0 2.2 copy-start.3
Sparse Core Ops, SparseCore 0:
  127.2 67.9 all-reduce.2
where the time goes:
time: 265 us; the launch traced here: 262 us
  local copies, waits for them, and re-layouts  196 us (74%)
  starting transfers between devices  25.1 us (9%)
  between operations  15.6 us (6%)
  other arithmetic  13.4 us (5%)
  matrix products  11.9 us (4%)
    unnamed x26, local copies, waits for them, and re-layouts  145 us
    all_to_all x2, local copies, waits for them, and re-layouts, per_device(): lax.all_to_all(outgoing[0], 'pw', split_axis=3, concat_axis=1, tiled=True)  31 us
    all_to_all x2, local copies, waits for them, and re-layouts, per_device(): lax.all_to_all(outgoing[1], 'pw', split_axis=3, concat_axis=1, tiled=True)  18.4 us
    all_to_all x1, starting transfers between devices, per_device(): lax.all_to_all(outgoing[0], 'pw', split_axis=3, concat_axis=1, tiled=True)  13.7 us
    dot_general x8, matrix products, rotate_plane(): lax.dot_general(panels[subspace_slab], block, (((0,), (0,)), ((), ())), p...  11.9 us
    all_to_all x1, starting transfers between devices, per_device(): lax.all_to_all(outgoing[1], 'pw', split_axis=3, concat_axis=1, tiled=True)  11.1 us
  transfers between devices with their start and end apart: 3, of which 0 were waited for; matrix products, arithmetic and copies ran while one was open for 61% of the time, Pallas kernels for 0%

commit v1 on v0

v1 whole, which is shorter than its diff:
```python
import functools

import jax
import jax.numpy as jnp
from jax import lax
from jax.experimental import pallas as pl
from jax.experimental.pallas import tpu as pltpu
from jax.sharding import PartitionSpec as P

GRID = 64
LANES = 128
ROWS = 16
STEPS = 256.0
TOP = 32600.0


def pack_body(r_ref, l_ref, out_ref):
    dests = out_ref.shape[0]
    stride = 2 * dests
    sources = [ref.reshape(ROWS * stride, LANES) for ref in (r_ref, l_ref)]
    lane = lax.broadcasted_iota(jnp.int32, (8, LANES), 1)
    for d in range(dests):
        codes = []
        for a, ref in enumerate(sources):
            halves = [ref[pl.ds(2 * d + p, ROWS, stride=stride), :] for p in range(2)]
            top = jnp.maximum(jnp.abs(halves[0]), jnp.abs(halves[1]))
            top = jnp.max(top, axis=1, keepdims=True)
            code = jnp.ceil(jnp.log2(jnp.maximum(top, 1e-30)) * STEPS) + 1.0
            inverse = jnp.exp2(code * (-1.0 / STEPS)) * TOP
            for p in range(2):
                q = jnp.round(halves[p] * inverse).astype(jnp.int32)
                at = p * 2 * ROWS + a * ROWS
                out_ref[d, at : at + ROWS, :] = q.astype(jnp.int16)
            codes += [code[:8], code[8:]]
        low = jnp.where(lane < 32, codes[0], codes[1])
        high = jnp.where(lane < 96, codes[2], codes[3])
        tile = jnp.where(lane < 64, low, high)
        out_ref[d, 4 * ROWS :, :] = tile.astype(jnp.int32).astype(jnp.int16)


def pack(residual, local_field, dests):
    block = pl.BlockSpec((ROWS, 32, LANES), lambda g: (0, g, 0))
    return pl.pallas_call(
        pack_body,
        grid=(dests // 16,),
        in_specs=[block, block],
        out_specs=pl.BlockSpec((16, 72, LANES), lambda g: (g, 0, 0)),
        out_shape=jax.ShapeDtypeStruct((dests, 72, LANES), jnp.int16),
        compiler_params=pltpu.CompilerParams(vmem_limit_bytes=32 << 20),
        name="pack",
    )(residual, local_field)


def conditional(options, step):
    for condition, source, to, sem in options:

        @pl.when(condition)
        def _():
            getattr(pltpu.make_async_copy(source, to, sem), step)()


def start_and_wait(options):
    conditional(options, "start")
    conditional(options, "wait")


def place_of(keeper, band):
    return jnp.where(keeper == band, 0, jnp.where(keeper == (band ^ 1), 1, 2))


def turn_body(slot, band_ref, keepers_ref, own_ref, twin_ref, out_ref, panel_ref, sem):
    tall = panel_ref.shape[0]
    band = band_ref[0]
    panel = (band & 1) ^ slot
    rows = pl.ds(pl.multiple_of(panel * tall, tall), tall)
    mine = place_of(keepers_ref[panel], band) == 0
    start_and_wait(
        [
            (mine, own_ref.at[rows], panel_ref, sem),
            (jnp.logical_not(mine), twin_ref.at[rows], panel_ref, sem),
        ]
    )
    out_ref[...] = panel_ref[...].T


def turn(slot, band, keepers, own, twin):
    anywhere = pl.BlockSpec(memory_space=pl.ANY)
    scalar = pl.BlockSpec(memory_space=pltpu.SMEM)
    rows, span = own.shape
    return pl.pallas_call(
        functools.partial(turn_body, slot),
        in_specs=[scalar, scalar, anywhere, anywhere],
        out_specs=pl.BlockSpec((span, rows // 2), lambda: (0, 0)),
        out_shape=jax.ShapeDtypeStruct((span, rows // 2), own.dtype),
        scratch_shapes=[pltpu.VMEM((rows // 2, span), own.dtype), pltpu.SemaphoreType.DMA],
        compiler_params=pltpu.CompilerParams(vmem_limit_bytes=16 << 20),
        name="turn",
    )(band, keepers, own, twin)


def kinetic_of(position):
    total = jnp.zeros(position.shape, jnp.int32)
    for index in (position >> 12, (position >> 6) & (GRID - 1), position & (GRID - 1)):
        folded = jnp.where(index >= GRID // 2, index - GRID, index)
        total = total + folded * folded
    return total.astype(jnp.float32) * (1.0 / (GRID * GRID))


def unpack(got_ref, hi_ref, lo_ref):
    sources = got_ref.shape[0]
    codes = got_ref[:, 4 * ROWS :, :].astype(jnp.int32).astype(jnp.float32)
    scales = jnp.exp2(codes * (1.0 / STEPS)) * (1.0 / TOP)
    for a in range(2):
        for p in range(2):
            at = p * 2 * ROWS + a * ROWS
            q = got_ref[:, at : at + ROWS, :].astype(jnp.int32).astype(jnp.float32)
            for r in range(2):
                col = 64 * a + 32 * r
                x = q[:, 8 * r : 8 * r + 8, :] * scales[:, :, col : col + 1]
                x = x.reshape(sources * 8, LANES)
                hi = x.astype(jnp.bfloat16)
                lo = (x - hi.astype(jnp.float32)).astype(jnp.bfloat16)
                hi_ref[a, r, :, p * LANES : (p + 1) * LANES] = hi
                lo_ref[a, r, :, p * LANES : (p + 1) * LANES] = lo


def rotate_body(
    band_ref, keepers_ref, lat_ref, got_ref, chip_ref, rest_ref, near_ref, far_ref, psi_ref, h_ref,
    psi_out, h_out, hi_ref, lo_ref, v_ref, state, v_sems, ins, outs
):
    planes, span, _ = psi_ref.shape
    tiles = outs.shape[1]
    tall = span // tiles
    depth = v_ref.shape[1] // 2

    band = band_ref[0]
    panels = []
    for p in range(2):
        here = place_of(keepers_ref[p], band) < 2
        to = v_ref.at[:, p * depth : (p + 1) * depth]
        for slot, refs in enumerate(((chip_ref, near_ref), (rest_ref, far_ref))):
            mine = (band & 1) ^ slot == p
            panels.append((mine & here, refs[0], to, v_sems.at[p]))
            panels.append((mine & jnp.logical_not(here), refs[1], to, v_sems.at[p]))

    def copies(refs, sems, inward):
        made = []
        for t in range(tiles):
            for s, ref in enumerate(refs):
                rows = pl.ds(t * tall, tall)
                ends = (ref.at[:, rows], state.at[s, :, rows])
                ends = ends if inward else ends[::-1]
                made.append(pltpu.make_async_copy(*ends, sems.at[s, t]))
        return made

    fetch = copies((psi_ref, h_ref), ins, True)
    store = copies((psi_out, h_out), outs, False)
    conditional(panels, "start")
    for copy in fetch:
        copy.start()
    kinetic = kinetic_of(lat_ref[...])
    unpack(got_ref, hi_ref, lo_ref)
    conditional(panels, "wait")
    for copy in fetch:
        copy.wait()
    for t in range(tiles):
        rows = slice(t * tall, (t + 1) * tall)
        v = v_ref[rows, :]

        def product(a, r):
            return jnp.dot(v, hi_ref[a, r], preferred_element_type=jnp.float32) + jnp.dot(
                v, lo_ref[a, r], preferred_element_type=jnp.float32
            )

        for r in range(planes):
            rotated = product(0, r)
            psi = state[0, r, rows].astype(jnp.float32)
            state[0, r, rows] = (psi + rotated).astype(jnp.bfloat16)
            applied = kinetic * rotated + product(1, r)
            h = state[1, r, rows].astype(jnp.float32)
            state[1, r, rows] = (h + applied).astype(jnp.bfloat16)
        store[2 * t].start()
        store[2 * t + 1].start()
    for copy in store:
        copy.wait()


def rotate(band, keepers, lattice, got, panels, psi, h):
    planes, span, width = psi.shape
    tiles = 8
    split = pltpu.VMEM((2, planes, got.shape[0] * 8, width), jnp.bfloat16)
    near = pl.BlockSpec(memory_space=pltpu.VMEM)
    far = pl.BlockSpec(memory_space=pl.ANY)
    scalar = pl.BlockSpec(memory_space=pltpu.SMEM)
    return pl.pallas_call(
        rotate_body,
        in_specs=[scalar, scalar, near, near] + [far] * 6,
        out_specs=[far, far],
        out_shape=[jax.ShapeDtypeStruct(psi.shape, psi.dtype)] * 2,
        scratch_shapes=[
            split,
            split,
            pltpu.VMEM((span, 2 * panels[0].shape[1]), panels[0].dtype),
            pltpu.VMEM((2,) + psi.shape, psi.dtype),
            pltpu.SemaphoreType.DMA((2,)),
            pltpu.SemaphoreType.DMA((2, tiles)),
            pltpu.SemaphoreType.DMA((2, tiles)),
        ],
        compiler_params=pltpu.CompilerParams(vmem_limit_bytes=52 << 20),
        name="rotate",
    )(band, keepers, lattice, got, *panels, psi, h)


def solution(mesh):
    n_pw = mesh.shape["pw"]
    n_band = mesh.shape["band"]

    def per_device(residual, local_field, orbital, energy, store, keepers, lattice):
        planes, vectors, _, waves = residual.shape
        width = waves // n_pw
        span = store.shape[2]
        band = lax.axis_index("band").reshape(1)

        swap = [(b, b ^ 1) for b in range(n_band)]
        across = [
            (p * n_band + b, (p ^ (n_pw // 2)) * n_band + (b ^ 2))
            for p in range(n_pw)
            for b in range(n_band)
        ]
        own = store[0]
        twin = lax.ppermute(own, "band", swap)
        chip = turn(0, band, keepers, own, twin)
        near = lax.ppermute(chip, ("pw", "band"), across)
        rest = turn(1, band, keepers, own, twin)
        far = lax.ppermute(near, "band", swap)

        rows = planes * vectors
        flat = (rows, waves // LANES, LANES)
        sent = pack(residual.reshape(flat), local_field.reshape(flat), n_pw)
        got = lax.all_to_all(sent, "pw", split_axis=0, concat_axis=0, tiled=True)

        shape = (planes, span, width)
        psi, h = rotate(
            band, keepers, lattice, got, (chip, rest, near, far), orbital.reshape(shape), energy.reshape(shape)
        )
        return psi.reshape(orbital.shape), h.reshape(energy.shape)

    in_specs = (
        P(None, "pw", "band", None),
        P(None, "pw", "band", None),
        P(None, None, "band", "pw"),
        P(None, None, "band", "pw"),
        P("band", None, None),
        P(),
        P("band", "pw"),
    )
    out_specs = (P(None, None, "band", "pw"), P(None, None, "band", "pw"))
    return jax.shard_map(
        per_device, mesh=mesh, in_specs=in_specs, out_specs=out_specs, check_vma=False
    )
```

time: 265 us -> 62.5 us (0.24); the launches traced: 262 us -> 61.8 us
  local copies, waits for them, and re-layouts: 196 us -> 3.43 us
  waiting for transfers between devices: 0.04 us -> 23 us
  Pallas kernels: 0 us -> 15.4 us
  between operations: 15.6 us -> 0.71 us
  other arithmetic: 13.4 us -> 0 us
  matrix products: 11.9 us -> 0 us
  starting transfers between devices: 25.1 us -> 19.4 us
    unnamed x26 -> x12, local copies, waits for them, and re-layouts: 145 us -> 3.43 us
    all_to_all x4 -> x0, local copies, waits for them, and re-layouts: 49.4 us -> none  [the longest x2 31 us: per_device(): lax.all_to_all(outgoing[0], 'pw', split_axis=3, concat_axis=1, tiled=True)]
    ppermute x0 -> x3, waiting for transfers between devices: none -> 22.9 us  [the longest x1 22.9 us: per_device(): near = lax.ppermute(chip, ('pw', 'band'), across)]
    pallas_call x0 -> x4, Pallas kernels: none -> 15.4 us  [the longest x1 9.36 us: rotate(): pl.pallas_call(rotate_body, in_specs=[scalar, scalar, near, near] + [far]...]
    all_to_all x2 -> x1, starting transfers between devices: 24.8 us -> 11.2 us  [per_device(): got = lax.all_to_all(sent, 'pw', split_axis=0, concat_axis=0, tiled=True)]
    dot_general x8 -> x0, matrix products: 11.9 us -> none  [rotate_plane(): lax.dot_general(panels[subspace_slab], block, (((0,), (0,)), ((), ())), p...]
    ppermute x0 -> x3, starting transfers between devices: none -> 8.15 us  [the longest x1 3.55 us: per_device(): near = lax.ppermute(chip, ('pw', 'band'), across)]
    all_to_all x2 -> x0, other arithmetic: 7.72 us -> none  [the longest x1 4.43 us: per_device(): lax.all_to_all(outgoing[1], 'pw', split_axis=3, concat_axis=1, tiled=True)]
  transfers between devices with their start and end apart: 3 -> 4, of which waited for: 0 -> 1; matrix products, arithmetic and copies ran while one was open for 61% -> 0% of each run, Pallas kernels for 0% -> 10%
where the time goes in v1:
time: 62.5 us; the launch traced here: 61.8 us
  waiting for transfers between devices  23 us (37%)
  starting transfers between devices  19.4 us (31%)
  Pallas kernels  15.4 us (25%)
  local copies, waits for them, and re-layouts  3.43 us (5%)
  between operations  0.71 us (1%)
    ppermute x1, waiting for transfers between devices, per_device(): near = lax.ppermute(chip, ('pw', 'band'), across)  22.9 us
    all_to_all x1, starting transfers between devices, per_device(): got = lax.all_to_all(sent, 'pw', split_axis=0, concat_axis=0, tiled=True)  11.2 us
    pallas_call x1, Pallas kernels, rotate(): pl.pallas_call(rotate_body, in_specs=[scalar, scalar, near, near] + [far]...  9.36 us
    ppermute x1, starting transfers between devices, per_device(): near = lax.ppermute(chip, ('pw', 'band'), across)  3.55 us
    unnamed x12, local copies, waits for them, and re-layouts  3.43 us
    ppermute x1, starting transfers between devices, per_device(): twin = lax.ppermute(own, 'band', swap)  3.33 us
    pallas_call x2, Pallas kernels, turn(): pl.pallas_call(functools.partial(turn_body, slot), in_specs=[scalar, scal...  3.07 us
    pallas_call x1, Pallas kernels, pack(): pl.pallas_call(pack_body, grid=(dests // 16,), in_specs=[block, block], o...  2.92 us
  transfers between devices with their start and end apart: 4, of which 1 were waited for; matrix products, arithmetic and copies ran while one was open for 0% of the time, Pallas kernels for 10%

profile of v1, /device:TPU:1, one launch (start us, length us, event | category | flops | bytes accessed | tf_op | source)
XLA Modules:
  0.0 61.8 jit_solution(13706008356193578265)
XLA Ops:
  0.6 3.3 %collective-permute-start = (bf16[512,2048]{1,0:T(8,128)(2,1)}, bf16[512,2048]{1,0:T(8,128)(2,1)}, u32[]{:S(2)}, u32[]{:S(2)}) collective-permute-start(bf16[512,2048]{1,0:T(8,128)(2,1)} %bitcast.12), channel_id=1, source_target_pairs={{0,1},{1,0},{2,3},{3,2},{4,5},{5,4},{6,7},{7,6},{8,9},{9,8},{10,11... | collective-permute-start | bytes 6291464 | tf_op jit(solution)/shard_map/ppermute | solution.py:231
  4.0 0.0 copy-start.2
  4.0 1.2 %copy-done.2 = f32[2,8,1,16384]{3,2,1,0:T(1,128)S(1)} copy-done((f32[2,8,1,16384]{3,2,1,0:T(1,128)S(1)}, f32[2,8,1,16384]{3,2,1,0:T(1,128)}, u32[]{:S(2)}) %copy-start.2) | copy-done | bytes 1048600
  5.2 0.0 copy-start.3
  5.2 1.2 %copy-done.3 = f32[2,8,1,16384]{3,2,1,0:T(1,128)S(1)} copy-done((f32[2,8,1,16384]{3,2,1,0:T(1,128)S(1)}, f32[2,8,1,16384]{3,2,1,0:T(1,128)}, u32[]{:S(2)}) %copy-start.3) | copy-done | bytes 1048600
  6.4 0.0 copy-start
  6.4 0.0 copy-start.4
  6.4 2.9 %pack.1 = s16[64,72,128]{2,1,0:T(8,128)(2,1)} custom-call(f32[16,128,128]{2,1,0:T(8,128)S(1)} %bitcast.15, f32[16,128,128]{2,1,0:T(8,128)S(1)} %bitcast.16), custom_call_target="tpu_custom_call" | custom-call | tf_op jit(solution)/shard_map/pack/pallas_call | solution.py:43
  9.3 11.2 %all-to-all-start = ((s16[64,72,128]{2,1,0:T(8,128)(2,1)}), s16[64,72,128]{2,1,0:T(8,128)(2,1)}, u32[]{:S(2)}, u32[]{:S(2)}) async-start(s16[64,72,128]{2,1,0:T(8,128)(2,1)} %pack.1), calls=%async_computation | async-start | bytes 2359296 | tf_op jit(solution)/shard_map/all_to_all | solution.py:240
  20.6 0.0 collective-permute-done.twin_ref
  20.6 0.0 copy-done
  20.6 0.0 copy-done.4
  20.6 1.0 %turn.2.chip_ref = bf16[2048,256]{1,0:T(8,128)(2,1)S(1)} custom-call(s32[1]{0:T(128)} %bitcast.band_ref, s32[2]{0:T(128)S(1)} %copy-done.4, bf16[512,2048]{1,0:T(8,128)(2,1)S(1)} %bitcast.13, bf16[512,2048]{1,0:T(8,128)(2,1)} %collective-permute-done.twin_ref), custom_call_target="tpu_custom_call" | custom-call | tf_op jit(solution)/shard_map/turn/pallas_call | solution.py:90
  21.6 0.0 copy-start.5
  21.6 3.6 %collective-permute-start.1 = (bf16[2048,256]{1,0:T(8,128)(2,1)S(1)}, bf16[2048,256]{1,0:T(8,128)(2,1)}, u32[]{:S(2)}, u32[]{:S(2)}) collective-permute-start(bf16[2048,256]{1,0:T(8,128)(2,1)S(1)} %turn.2.chip_ref), channel_id=1, source_target_pairs={{0,130},{1,131},{2,128},{3,129},{4,134},{5,135},{6,132},{7,133},{8... | collective-permute-start | bytes 3145736 | tf_op jit(solution)/shard_map/ppermute | solution.py:233
  25.2 22.9 %collective-permute-done.1.near_ref = bf16[2048,256]{1,0:T(8,128)(2,1)} collective-permute-done((bf16[2048,256]{1,0:T(8,128)(2,1)S(1)}, bf16[2048,256]{1,0:T(8,128)(2,1)}, u32[]{:S(2)}, u32[]{:S(2)}) %collective-permute-start.1) | collective-permute-done | bytes 1048608 | tf_op jit(solution)/shard_map/ppermute | solution.py:233
  48.1 1.3 %collective-permute-start.2 = (bf16[2048,256]{1,0:T(8,128)(2,1)}, bf16[2048,256]{1,0:T(8,128)(2,1)}, u32[]{:S(2)}, u32[]{:S(2)}) collective-permute-start(bf16[2048,256]{1,0:T(8,128)(2,1)} %collective-permute-done.1.near_ref), channel_id=1, source_target_pairs={{0,1},{1,0},{2,3},{3,2},{4,5},{5,4},{6,7},{7,6},{8,9},{9,8},{10,11... | collective-permute-start | bytes 3145736 | tf_op jit(solution)/shard_map/ppermute | solution.py:235
  49.4 2.1 %turn.3.rest_ref = bf16[2048,256]{1,0:T(8,128)(2,1)S(1)} custom-call(s32[1]{0:T(128)} %bitcast.band_ref, s32[2]{0:T(128)S(1)} %copy-done.4, bf16[512,2048]{1,0:T(8,128)(2,1)S(1)} %bitcast.14, bf16[512,2048]{1,0:T(8,128)(2,1)} %collective-permute-done.twin_ref), custom_call_target="tpu_custom_call" | custom-call | tf_op jit(solution)/shard_map/turn/pallas_call | solution.py:90
  51.5 0.0 copy-start.1
  51.5 1.0 %copy-done.1 = bf16[2048,256]{1,0:T(8,128)(2,1)} copy-done((bf16[2048,256]{1,0:T(8,128)(2,1)}, bf16[2048,256]{1,0:T(8,128)(2,1)S(1)}, u32[]{:S(2)}) %copy-start.1) | copy-done | bytes 1048600
  52.5 0.0 all-to-all-done.got_ref
  52.5 0.0 collective-permute-done.2.far_ref
  52.5 0.0 copy-done.5
  52.5 9.4 %rotate.1 = (bf16[2,2048,256]{2,1,0:T(8,128)(2,1)}, bf16[2,2048,256]{2,1,0:T(8,128)(2,1)}) custom-call(s32[1]{0:T(128)} %bitcast.band_ref, s32[2]{0:T(128)S(1)} %copy-done.4, s32[1,256]{1,0:T(1,128)S(1)} %copy-done.5, s16[64,72,128]{2,1,0:T(8,128)(2,1)} %all-to-all-done.got_ref, bf16[2048,256]{1,0:T(8,128)(2,1)S(1)} %turn.2.chip_ref, ...), custom_call_target="tpu_custom_call" | custom-call | tf_op jit(solution)/shard_map/rotate/pallas_call | solution.py:195
Async XLA Ops:
  0.6 20.0 %collective-permute-start = (bf16[512,2048]{1,0:T(8,128)(2,1)}, bf16[512,2048]{1,0:T(8,128)(2,1)}, u32[]{:S(2)}, u32[]{:S(2)}) collective-permute-start(bf16[512,2048]{1,0:T(8,128)(2,1)} %bitcast.12), channel_id=1, source_target_pairs={{0,1},{1,0},{2,3},{3,2},{4,5},{5,4},{6,7},{7,6},{8,9},{9,8},{10,11... | collective-permute-start | bytes 6291464 | tf_op jit(solution)/shard_map/ppermute | solution.py:231
  4.0 1.2 %copy-start.2 = (f32[2,8,1,16384]{3,2,1,0:T(1,128)S(1)}, f32[2,8,1,16384]{3,2,1,0:T(1,128)}, u32[]{:S(2)}) copy-start(f32[2,8,1,16384]{3,2,1,0:T(1,128)} %param.7) | copy-start | bytes 3145732
  5.2 1.2 %copy-start.3 = (f32[2,8,1,16384]{3,2,1,0:T(1,128)S(1)}, f32[2,8,1,16384]{3,2,1,0:T(1,128)}, u32[]{:S(2)}) copy-start(f32[2,8,1,16384]{3,2,1,0:T(1,128)} %param.8) | copy-start | bytes 3145732
  6.4 14.2 %copy-start = (bf16[1,512,2048]{2,1,0:T(8,128)(2,1)S(1)}, bf16[1,512,2048]{2,1,0:T(8,128)(2,1)}, u32[]{:S(2)}) copy-start(bf16[1,512,2048]{2,1,0:T(8,128)(2,1)} %param.11) | copy-start | bytes 6291460
  6.4 14.2 %copy-start.4 = (s32[2]{0:T(128)S(1)}, s32[2]{0:T(128)}, u32[]{:S(2)}) copy-start(s32[2]{0:T(128)} %keepers_ref.5) | copy-start | bytes 28
  9.3 43.1 %all-to-all-start = ((s16[64,72,128]{2,1,0:T(8,128)(2,1)}), s16[64,72,128]{2,1,0:T(8,128)(2,1)}, u32[]{:S(2)}, u32[]{:S(2)}) async-start(s16[64,72,128]{2,1,0:T(8,128)(2,1)} %pack.1), calls=%async_computation | async-start | bytes 2359296 | tf_op jit(solution)/shard_map/all_to_all | solution.py:240
  21.6 30.9 %copy-start.5 = (s32[1,256]{1,0:T(1,128)S(1)}, s32[1,256]{1,0:T(1,128)}, u32[]{:S(2)}) copy-start(s32[1,256]{1,0:T(1,128)} %lat_ref.1) | copy-start | bytes 3076
  21.6 26.5 %collective-permute-start.1 = (bf16[2048,256]{1,0:T(8,128)(2,1)S(1)}, bf16[2048,256]{1,0:T(8,128)(2,1)}, u32[]{:S(2)}, u32[]{:S(2)}) collective-permute-start(bf16[2048,256]{1,0:T(8,128)(2,1)S(1)} %turn.2.chip_ref), channel_id=1, source_target_pairs={{0,130},{1,131},{2,128},{3,129},{4,134},{5,135},{6,132},{7,133},{8... | collective-permute-start | bytes 3145736 | tf_op jit(solution)/shard_map/ppermute | solution.py:233
  48.1 4.4 %collective-permute-start.2 = (bf16[2048,256]{1,0:T(8,128)(2,1)}, bf16[2048,256]{1,0:T(8,128)(2,1)}, u32[]{:S(2)}, u32[]{:S(2)}) collective-permute-start(bf16[2048,256]{1,0:T(8,128)(2,1)} %collective-permute-done.1.near_ref), channel_id=1, source_target_pairs={{0,1},{1,0},{2,3},{3,2},{4,5},{5,4},{6,7},{7,6},{8,9},{9,8},{10,11... | collective-permute-start | bytes 3145736 | tf_op jit(solution)/shard_map/ppermute | solution.py:235
  51.5 1.0 %copy-start.1 = (bf16[2048,256]{1,0:T(8,128)(2,1)}, bf16[2048,256]{1,0:T(8,128)(2,1)S(1)}, u32[]{:S(2)}) copy-start(bf16[2048,256]{1,0:T(8,128)(2,1)S(1)} %turn.3.rest_ref) | copy-start | bytes 3145732

commit v2 on v1

--- a/solution.py
+++ b/solution.py
@@ -12,41 +12,71 @@
 ROWS = 16
 STEPS = 256.0
 TOP = 32600.0
-
-
-def pack_body(r_ref, l_ref, out_ref):
-    dests = out_ref.shape[0]
+TILES = (640, 640, 512, 256)
+
+
+def pack_body(r_ref, l_ref, out_ref, fields, sent, ins, outs):
+    chunks = outs.shape[0]
+    dests = sent.shape[0] // chunks
     stride = 2 * dests
-    sources = [ref.reshape(ROWS * stride, LANES) for ref in (r_ref, l_ref)]
+
+    fetch = [
+        [
+            pltpu.make_async_copy(ref.at[:, pl.ds(c * stride, stride)], fields.at[c, a], ins.at[c, a])
+            for a, ref in enumerate((r_ref, l_ref))
+        ]
+        for c in range(chunks)
+    ]
+    store = []
+    for c in range(chunks):
+        for copy in fetch[c]:
+            copy.start()
+        some = pl.ds(c * dests, dests)
+        store.append(pltpu.make_async_copy(sent.at[some], out_ref.at[some], outs.at[c]))
+
     lane = lax.broadcasted_iota(jnp.int32, (8, LANES), 1)
-    for d in range(dests):
-        codes = []
-        for a, ref in enumerate(sources):
-            halves = [ref[pl.ds(2 * d + p, ROWS, stride=stride), :] for p in range(2)]
-            top = jnp.maximum(jnp.abs(halves[0]), jnp.abs(halves[1]))
-            top = jnp.max(top, axis=1, keepdims=True)
-            code = jnp.ceil(jnp.log2(jnp.maximum(top, 1e-30)) * STEPS) + 1.0
-            inverse = jnp.exp2(code * (-1.0 / STEPS)) * TOP
-            for p in range(2):
-                q = jnp.round(halves[p] * inverse).astype(jnp.int32)
-                at = p * 2 * ROWS + a * ROWS
-                out_ref[d, at : at + ROWS, :] = q.astype(jnp.int16)
-            codes += [code[:8], code[8:]]
-        low = jnp.where(lane < 32, codes[0], codes[1])
-        high = jnp.where(lane < 96, codes[2], codes[3])
-        tile = jnp.where(lane < 64, low, high)
-        out_ref[d, 4 * ROWS :, :] = tile.astype(jnp.int32).astype(jnp.int16)
+    for c in range(chunks):
+        for copy in fetch[c]:
+            copy.wait()
+        for d in range(dests):
+            codes = []
+            for a in range(2):
+                ref = fields.at[c, a].reshape(ROWS * stride, LANES)
+                halves = [ref[pl.ds(2 * d + p, ROWS, stride=stride), :] for p in range(2)]
+                top = jnp.maximum(jnp.abs(halves[0]), jnp.abs(halves[1]))
+                top = jnp.max(top, axis=1, keepdims=True)
+                code = jnp.ceil(jnp.log2(jnp.maximum(top, 1e-30)) * STEPS) + 1.0
+                inverse = jnp.exp2(code * (-1.0 / STEPS)) * TOP
+                for p in range(2):
+                    q = jnp.round(halves[p] * inverse).astype(jnp.int32)
+                    at = p * 2 * ROWS + a * ROWS
+                    sent[c * dests + d, at : at + ROWS, :] = q.astype(jnp.int16)
+                codes += [code[:8], code[8:]]
+            low = jnp.where(lane < 32, codes[0], codes[1])
+            high = jnp.where(lane < 96, codes[2], codes[3])
+            tile = jnp.where(lane < 64, low, high)
+            sent[c * dests + d, 4 * ROWS :, :] = tile.astype(jnp.int32).astype(jnp.int16)
+        store[c].start()
+    for copy in store:
+        copy.wait()
 
 
 def pack(residual, local_field, dests):
-    block = pl.BlockSpec((ROWS, 32, LANES), lambda g: (0, g, 0))
+    chunks = 8
+    anywhere = pl.BlockSpec(memory_space=pl.ANY)
+    rows = residual.shape[1] // chunks
     return pl.pallas_call(
         pack_body,
-        grid=(dests // 16,),
-        in_specs=[block, block],
-        out_specs=pl.BlockSpec((16, 72, LANES), lambda g: (g, 0, 0)),
+        in_specs=[anywhere, anywhere],
+        out_specs=anywhere,
         out_shape=jax.ShapeDtypeStruct((dests, 72, LANES), jnp.int16),
-        compiler_params=pltpu.CompilerParams(vmem_limit_bytes=32 << 20),
+        scratch_shapes=[
+            pltpu.VMEM((chunks, 2, ROWS, rows, LANES), jnp.float32),
+            pltpu.VMEM((dests, 72, LANES), jnp.int16),
+            pltpu.SemaphoreType.DMA((chunks, 2)),
+            pltpu.SemaphoreType.DMA((chunks,)),
+        ],
+        compiler_params=pltpu.CompilerParams(vmem_limit_bytes=58 << 20),
         name="pack",
     )(residual, local_field)
 
@@ -125,29 +155,33 @@
 
 
 def rotate_body(
-    band_ref, keepers_ref, lat_ref, got_ref, chip_ref, rest_ref, near_ref, far_ref, psi_ref, h_ref,
-    psi_out, h_out, hi_ref, lo_ref, v_ref, state, v_sems, ins, outs
+    band_ref, keepers_ref, lat_ref, got_hbm, chip_ref, rest_ref, near_ref, far_ref, psi_ref, h_ref,
+    psi_out, h_out, got_ref, hi_ref, lo_ref, v_ref, state, got_sem, v_sems, ins, outs
 ):
-    planes, span, _ = psi_ref.shape
-    tiles = outs.shape[1]
-    tall = span // tiles
+    tiles = len(TILES)
+    starts = [sum(TILES[:t]) for t in range(tiles)]
+    planes = psi_ref.shape[0]
     depth = v_ref.shape[1] // 2
 
     band = band_ref[0]
     panels = []
-    for p in range(2):
-        here = place_of(keepers_ref[p], band) < 2
-        to = v_ref.at[:, p * depth : (p + 1) * depth]
-        for slot, refs in enumerate(((chip_ref, near_ref), (rest_ref, far_ref))):
-            mine = (band & 1) ^ slot == p
-            panels.append((mine & here, refs[0], to, v_sems.at[p]))
-            panels.append((mine & jnp.logical_not(here), refs[1], to, v_sems.at[p]))
+    for t in range(tiles):
+        rows = pl.ds(starts[t], TILES[t])
+        options = []
+        for p in range(2):
+            here = place_of(keepers_ref[p], band) < 2
+            to = v_ref.at[rows, p * depth : (p + 1) * depth]
+            for slot, refs in enumerate(((chip_ref, near_ref), (rest_ref, far_ref))):
+                mine = (band & 1) ^ slot == p
+                options.append((mine & here, refs[0].at[rows], to, v_sems.at[t, p]))
+                options.append((mine & jnp.logical_not(here), refs[1].at[rows], to, v_sems.at[t, p]))
+        panels.append(options)
 
     def copies(refs, sems, inward):
         made = []
         for t in range(tiles):
             for s, ref in enumerate(refs):
-                rows = pl.ds(t * tall, tall)
+                rows = pl.ds(starts[t], TILES[t])
                 ends = (ref.at[:, rows], state.at[s, :, rows])
                 ends = ends if inward else ends[::-1]
                 made.append(pltpu.make_async_copy(*ends, sems.at[s, t]))
@@ -155,16 +189,20 @@
 
     fetch = copies((psi_ref, h_ref), ins, True)
     store = copies((psi_out, h_out), outs, False)
-    conditional(panels, "start")
-    for copy in fetch:
-        copy.start()
+    message = pltpu.make_async_copy(got_hbm, got_ref, got_sem)
+    message.start()
+    for t in range(tiles):
+        conditional(panels[t], "start")
+        for s in range(2):
+            fetch[2 * t + s].start()
     kinetic = kinetic_of(lat_ref[...])
+    message.wait()
     unpack(got_ref, hi_ref, lo_ref)
-    conditional(panels, "wait")
-    for copy in fetch:
-        copy.wait()
     for t in range(tiles):
-        rows = slice(t * tall, (t + 1) * tall)
+        conditional(panels[t], "wait")
+        for s in range(2):
+            fetch[2 * t + s].wait()
+        rows = slice(starts[t], starts[t] + TILES[t])
         v = v_ref[rows, :]
 
         def product(a, r):
@@ -187,22 +225,25 @@
 
 def rotate(band, keepers, lattice, got, panels, psi, h):
     planes, span, width = psi.shape
-    tiles = 8
+    assert sum(TILES) == span
+    tiles = len(TILES)
     split = pltpu.VMEM((2, planes, got.shape[0] * 8, width), jnp.bfloat16)
     near = pl.BlockSpec(memory_space=pltpu.VMEM)
     far = pl.BlockSpec(memory_space=pl.ANY)
     scalar = pl.BlockSpec(memory_space=pltpu.SMEM)
     return pl.pallas_call(
         rotate_body,
-        in_specs=[scalar, scalar, near, near] + [far] * 6,
+        in_specs=[scalar, scalar, near] + [far] * 7,
         out_specs=[far, far],
         out_shape=[jax.ShapeDtypeStruct(psi.shape, psi.dtype)] * 2,
         scratch_shapes=[
+            pltpu.VMEM(got.shape, got.dtype),
             split,
             split,
             pltpu.VMEM((span, 2 * panels[0].shape[1]), panels[0].dtype),
             pltpu.VMEM((2,) + psi.shape, psi.dtype),
-            pltpu.SemaphoreType.DMA((2,)),
+            pltpu.SemaphoreType.DMA,
+            pltpu.SemaphoreType.DMA((tiles, 2)),
             pltpu.SemaphoreType.DMA((2, tiles)),
             pltpu.SemaphoreType.DMA((2, tiles)),
         ],

time: 62.5 us -> 59.2 us (0.947)
  local copies, waits for them, and re-layouts: 3.43 us -> 0.97 us
  Pallas kernels: 15.4 us -> 13.8 us
    unnamed x12 -> x8, local copies, waits for them, and re-layouts: 3.43 us -> 0.97 us
    pallas_call x2, Pallas kernels: 3.07 us -> 1.92 us  [turn(): pl.pallas_call(functools.partial(turn_body, slot), in_specs=[scalar, scal...]
    ppermute x1, waiting for transfers between devices: 0.01 us -> 0.7 us  [per_device(): far = lax.ppermute(near, 'band', swap)]
  transfers between devices with their start and end apart: 4 -> 4, of which waited for: 1 -> 2; matrix products, arithmetic and copies ran while one was open for 0% -> 0% of each run, Pallas kernels for 10% -> 9%
where the time goes in v2:
time: 59.2 us; the launch traced here: 58.5 us
  waiting for transfers between devices  23.4 us (40%)
  starting transfers between devices  19.7 us (33%)
  Pallas kernels  13.8 us (23%)
  local copies, waits for them, and re-layouts  0.97 us (2%)
  between operations  0.71 us (1%)
    ppermute x1, waiting for transfers between devices, per_device(): near = lax.ppermute(chip, ('pw', 'band'), across)  22.7 us
    all_to_all x1, starting transfers between devices, per_device(): got = lax.all_to_all(sent, 'pw', split_axis=0, concat_axis=0, tiled=True)  11.3 us
    pallas_call x1, Pallas kernels, rotate(): pl.pallas_call(rotate_body, in_specs=[scalar, scalar, near] + [far] * 7,...  8.47 us
    ppermute x1, starting transfers between devices, per_device(): near = lax.ppermute(chip, ('pw', 'band'), across)  3.55 us
    pallas_call x1, Pallas kernels, pack(): pl.pallas_call(pack_body, in_specs=[anywhere, anywhere], out_specs=anywhe...  3.4 us
    ppermute x1, starting transfers between devices, per_device(): twin = lax.ppermute(own, 'band', swap)  3.33 us
    pallas_call x2, Pallas kernels, turn(): pl.pallas_call(functools.partial(turn_body, slot), in_specs=[scalar, scal...  1.92 us
    ppermute x1, starting transfers between devices, per_device(): far = lax.ppermute(near, 'band', swap)  1.54 us
  transfers between devices with their start and end apart: 4, of which 2 were waited for; matrix products, arithmetic and copies ran while one was open for 0% of the time, Pallas kernels for 9%

profile of v2, /device:TPU:1, one launch (start us, length us, event | category | flops | bytes accessed | tf_op | source)
XLA Modules:
  0.0 58.5 jit_solution(15886707162303564303)
XLA Ops:
  0.6 3.3 %collective-permute-start = (bf16[512,2048]{1,0:T(8,128)(2,1)}, bf16[512,2048]{1,0:T(8,128)(2,1)}, u32[]{:S(2)}, u32[]{:S(2)}) collective-permute-start(bf16[512,2048]{1,0:T(8,128)(2,1)} %bitcast.12), channel_id=1, source_target_pairs={{0,1},{1,0},{2,3},{3,2},{4,5},{5,4},{6,7},{7,6},{8,9},{9,8},{10,11... | collective-permute-start | bytes 6291464 | tf_op jit(solution)/shard_map/ppermute | solution.py:272
  4.0 0.0 copy-start
  4.0 0.0 copy-start.2
  4.0 3.4 %pack.1 = s16[64,72,128]{2,1,0:T(8,128)(2,1)} custom-call(f32[16,128,128]{2,1,0:T(8,128)} %bitcast.17, f32[16,128,128]{2,1,0:T(8,128)} %bitcast.18), custom_call_target="tpu_custom_call" | custom-call | tf_op jit(solution)/shard_map/pack/pallas_call | solution.py:68
  7.4 11.3 %all-to-all-start = ((s16[64,72,128]{2,1,0:T(8,128)(2,1)}), s16[64,72,128]{2,1,0:T(8,128)(2,1)}, u32[]{:S(2)}, u32[]{:S(2)}) async-start(s16[64,72,128]{2,1,0:T(8,128)(2,1)} %pack.1), calls=%async_computation | async-start | bytes 2359296 | tf_op jit(solution)/shard_map/all_to_all | solution.py:281
  18.6 0.0 collective-permute-done.twin_ref
  18.7 0.0 copy-done
  18.7 0.0 copy-done.2
  18.7 1.0 %turn.2.chip_ref = bf16[2048,256]{1,0:T(8,128)(2,1)S(1)} custom-call(s32[1]{0:T(128)} %bitcast.band_ref, s32[2]{0:T(128)S(1)} %copy-done.2, bf16[512,2048]{1,0:T(8,128)(2,1)S(1)} %bitcast.13, bf16[512,2048]{1,0:T(8,128)(2,1)} %collective-permute-done.twin_ref), custom_call_target="tpu_custom_call" | custom-call | tf_op jit(solution)/shard_map/turn/pallas_call | solution.py:120
  19.6 0.0 copy-start.3
  19.7 3.6 %collective-permute-start.1 = (bf16[2048,256]{1,0:T(8,128)(2,1)S(1)}, bf16[2048,256]{1,0:T(8,128)(2,1)}, u32[]{:S(2)}, u32[]{:S(2)}) collective-permute-start(bf16[2048,256]{1,0:T(8,128)(2,1)S(1)} %turn.2.chip_ref), channel_id=1, source_target_pairs={{0,130},{1,131},{2,128},{3,129},{4,134},{5,135},{6,132},{7,133},{8... | collective-permute-start | bytes 3145736 | tf_op jit(solution)/shard_map/ppermute | solution.py:274
  23.2 22.7 %collective-permute-done.1.near_ref = bf16[2048,256]{1,0:T(8,128)(2,1)} collective-permute-done((bf16[2048,256]{1,0:T(8,128)(2,1)S(1)}, bf16[2048,256]{1,0:T(8,128)(2,1)}, u32[]{:S(2)}, u32[]{:S(2)}) %collective-permute-start.1) | collective-permute-done | bytes 1048608 | tf_op jit(solution)/shard_map/ppermute | solution.py:274
  45.9 1.5 %collective-permute-start.2 = (bf16[2048,256]{1,0:T(8,128)(2,1)}, bf16[2048,256]{1,0:T(8,128)(2,1)}, u32[]{:S(2)}, u32[]{:S(2)}) collective-permute-start(bf16[2048,256]{1,0:T(8,128)(2,1)} %collective-permute-done.1.near_ref), channel_id=1, source_target_pairs={{0,1},{1,0},{2,3},{3,2},{4,5},{5,4},{6,7},{7,6},{8,9},{9,8},{10,11... | collective-permute-start | bytes 3145736 | tf_op jit(solution)/shard_map/ppermute | solution.py:276
  47.4 1.0 %turn.3.rest_ref = bf16[2048,256]{1,0:T(8,128)(2,1)S(1)} custom-call(s32[1]{0:T(128)} %bitcast.band_ref, s32[2]{0:T(128)S(1)} %copy-done.2, bf16[512,2048]{1,0:T(8,128)(2,1)S(1)} %bitcast.14, bf16[512,2048]{1,0:T(8,128)(2,1)} %collective-permute-done.twin_ref), custom_call_target="tpu_custom_call" | custom-call | tf_op jit(solution)/shard_map/turn/pallas_call | solution.py:120
  48.4 0.0 copy-start.1
  48.4 1.0 %copy-done.1 = bf16[2048,256]{1,0:T(8,128)(2,1)} copy-done((bf16[2048,256]{1,0:T(8,128)(2,1)}, bf16[2048,256]{1,0:T(8,128)(2,1)S(1)}, u32[]{:S(2)}) %copy-start.1) | copy-done | bytes 1048600
  49.4 0.0 all-to-all-done.got_hbm
  49.4 0.7 %collective-permute-done.2.far_ref = bf16[2048,256]{1,0:T(8,128)(2,1)} collective-permute-done((bf16[2048,256]{1,0:T(8,128)(2,1)}, bf16[2048,256]{1,0:T(8,128)(2,1)}, u32[]{:S(2)}, u32[]{:S(2)}) %collective-permute-start.2) | collective-permute-done | bytes 1048608 | tf_op jit(solution)/shard_map/ppermute | solution.py:276
  50.1 0.0 copy-done.3
  50.1 8.5 %rotate.1 = (bf16[2,2048,256]{2,1,0:T(8,128)(2,1)}, bf16[2,2048,256]{2,1,0:T(8,128)(2,1)}) custom-call(s32[1]{0:T(128)} %bitcast.band_ref, s32[2]{0:T(128)S(1)} %copy-done.2, s32[1,256]{1,0:T(1,128)S(1)} %copy-done.3, s16[64,72,128]{2,1,0:T(8,128)(2,1)} %all-to-all-done.got_hbm, bf16[2048,256]{1,0:T(8,128)(2,1)S(1)} %turn.2.chip_ref, ...), custom_call_target="tpu_custom_call" | custom-call | tf_op jit(solution)/shard_map/rotate/pallas_call | solution.py:234
Async XLA Ops:
  0.6 18.0 %collective-permute-start = (bf16[512,2048]{1,0:T(8,128)(2,1)}, bf16[512,2048]{1,0:T(8,128)(2,1)}, u32[]{:S(2)}, u32[]{:S(2)}) collective-permute-start(bf16[512,2048]{1,0:T(8,128)(2,1)} %bitcast.12), channel_id=1, source_target_pairs={{0,1},{1,0},{2,3},{3,2},{4,5},{5,4},{6,7},{7,6},{8,9},{9,8},{10,11... | collective-permute-start | bytes 6291464 | tf_op jit(solution)/shard_map/ppermute | solution.py:272
  4.0 14.7 %copy-start = (bf16[1,512,2048]{2,1,0:T(8,128)(2,1)S(1)}, bf16[1,512,2048]{2,1,0:T(8,128)(2,1)}, u32[]{:S(2)}) copy-start(bf16[1,512,2048]{2,1,0:T(8,128)(2,1)} %param.11) | copy-start | bytes 6291460
  4.0 14.7 %copy-start.2 = (s32[2]{0:T(128)S(1)}, s32[2]{0:T(128)}, u32[]{:S(2)}) copy-start(s32[2]{0:T(128)} %keepers_ref.5) | copy-start | bytes 28
  7.4 42.0 %all-to-all-start = ((s16[64,72,128]{2,1,0:T(8,128)(2,1)}), s16[64,72,128]{2,1,0:T(8,128)(2,1)}, u32[]{:S(2)}, u32[]{:S(2)}) async-start(s16[64,72,128]{2,1,0:T(8,128)(2,1)} %pack.1), calls=%async_computation | async-start | bytes 2359296 | tf_op jit(solution)/shard_map/all_to_all | solution.py:281
  19.6 30.4 %copy-start.3 = (s32[1,256]{1,0:T(1,128)S(1)}, s32[1,256]{1,0:T(1,128)}, u32[]{:S(2)}) copy-start(s32[1,256]{1,0:T(1,128)} %lat_ref.1) | copy-start | bytes 3076
  19.7 26.2 %collective-permute-start.1 = (bf16[2048,256]{1,0:T(8,128)(2,1)S(1)}, bf16[2048,256]{1,0:T(8,128)(2,1)}, u32[]{:S(2)}, u32[]{:S(2)}) collective-permute-start(bf16[2048,256]{1,0:T(8,128)(2,1)S(1)} %turn.2.chip_ref), channel_id=1, source_target_pairs={{0,130},{1,131},{2,128},{3,129},{4,134},{5,135},{6,132},{7,133},{8... | collective-permute-start | bytes 3145736 | tf_op jit(solution)/shard_map/ppermute | solution.py:274
  45.9 4.2 %collective-permute-start.2 = (bf16[2048,256]{1,0:T(8,128)(2,1)}, bf16[2048,256]{1,0:T(8,128)(2,1)}, u32[]{:S(2)}, u32[]{:S(2)}) collective-permute-start(bf16[2048,256]{1,0:T(8,128)(2,1)} %collective-permute-done.1.near_ref), channel_id=1, source_target_pairs={{0,1},{1,0},{2,3},{3,2},{4,5},{5,4},{6,7},{7,6},{8,9},{9,8},{10,11... | collective-permute-start | bytes 3145736 | tf_op jit(solution)/shard_map/ppermute | solution.py:276
  48.4 1.0 %copy-start.1 = (bf16[2048,256]{1,0:T(8,128)(2,1)}, bf16[2048,256]{1,0:T(8,128)(2,1)S(1)}, u32[]{:S(2)}) copy-start(bf16[2048,256]{1,0:T(8,128)(2,1)S(1)} %turn.3.rest_ref) | copy-start | bytes 3145732

commit v3 on v2

--- a/solution.py
+++ b/solution.py
@@ -123,7 +123,7 @@
         out_specs=pl.BlockSpec((span, rows // 2), lambda: (0, 0)),
         out_shape=jax.ShapeDtypeStruct((span, rows // 2), own.dtype),
         scratch_shapes=[pltpu.VMEM((rows // 2, span), own.dtype), pltpu.SemaphoreType.DMA],
-        compiler_params=pltpu.CompilerParams(vmem_limit_bytes=16 << 20),
+        compiler_params=pltpu.CompilerParams(vmem_limit_bytes=(16 if slot == 0 else 58) << 20),
         name="turn",
     )(band, keepers, own, twin)
 
@@ -273,6 +273,7 @@
         chip = turn(0, band, keepers, own, twin)
         near = lax.ppermute(chip, ("pw", "band"), across)
         rest = turn(1, band, keepers, own, twin)
+        near, rest = lax.optimization_barrier((near, rest))
         far = lax.ppermute(near, "band", swap)
 
         rows = planes * vectors

time: 59.2 us -> 58.9 us (level)
  Pallas kernels: 13.8 us -> 17.2 us
  starting transfers between devices: 19.7 us -> 17.6 us
  local copies, waits for them, and re-layouts: 0.97 us -> 0.02 us
    pallas_call x2, Pallas kernels: 1.92 us -> 5.34 us  [turn(): pl.pallas_call(functools.partial(turn_body, slot), in_specs=[scalar, scal...]
    ppermute x1, waiting for transfers between devices: 22.7 us -> 20.6 us  [per_device(): near = lax.ppermute(chip, ('pw', 'band'), across)]
    ppermute x1, waiting for transfers between devices: 0.7 us -> 2.07 us  [per_device(): far = lax.ppermute(near, 'band', swap)]
    ppermute x1, starting transfers between devices: 3.55 us -> 2.4 us  [per_device(): near = lax.ppermute(chip, ('pw', 'band'), across)]
    unnamed x8 -> x10, local copies, waits for them, and re-layouts: 0.97 us -> 0.02 us
    ppermute x1, starting transfers between devices: 1.54 us -> 0.62 us  [per_device(): far = lax.ppermute(near, 'band', swap)]
  transfers between devices with their start and end apart: 4 -> 4, of which waited for: 2 -> 3; matrix products, arithmetic and copies ran while one was open for 0% -> 0% of each run, Pallas kernels for 9% -> 15%
where the time goes in v3:
time: 58.9 us; the launch traced here: 58.6 us
  waiting for transfers between devices  23 us (39%)
  starting transfers between devices  17.6 us (30%)
  Pallas kernels  17.2 us (29%)
  between operations  0.71 us (1%)
    ppermute x1, waiting for transfers between devices, per_device(): near = lax.ppermute(chip, ('pw', 'band'), across)  20.6 us
    all_to_all x1, starting transfers between devices, per_device(): got = lax.all_to_all(sent, 'pw', split_axis=0, concat_axis=0, tiled=True)  11.3 us
    pallas_call x1, Pallas kernels, rotate(): pl.pallas_call(rotate_body, in_specs=[scalar, scalar, near] + [far] * 7,...  8.47 us
    pallas_call x2, Pallas kernels, turn(): pl.pallas_call(functools.partial(turn_body, slot), in_specs=[scalar, scal...  5.34 us
    pallas_call x1, Pallas kernels, pack(): pl.pallas_call(pack_body, in_specs=[anywhere, anywhere], out_specs=anywhe...  3.4 us
    ppermute x1, starting transfers between devices, per_device(): twin = lax.ppermute(own, 'band', swap)  3.33 us
    ppermute x1, starting transfers between devices, per_device(): near = lax.ppermute(chip, ('pw', 'band'), across)  2.4 us
    ppermute x1, waiting for transfers between devices, per_device(): far = lax.ppermute(near, 'band', swap)  2.07 us
  transfers between devices with their start and end apart: 4, of which 3 were waited for; matrix products, arithmetic and copies ran while one was open for 0% of the time, Pallas kernels for 15%

profile of v3, /device:TPU:1, one launch (start us, length us, event | category | flops | bytes accessed | tf_op | source)
XLA Modules:
  0.0 58.6 jit_solution(17959265646501538431)
XLA Ops:
  0.6 3.3 %collective-permute-start = (bf16[512,2048]{1,0:T(8,128)(2,1)}, bf16[512,2048]{1,0:T(8,128)(2,1)}, u32[]{:S(2)}, u32[]{:S(2)}) collective-permute-start(bf16[512,2048]{1,0:T(8,128)(2,1)} %bitcast.12), channel_id=1, source_target_pairs={{0,1},{1,0},{2,3},{3,2},{4,5},{5,4},{6,7},{7,6},{8,9},{9,8},{10,11... | collective-permute-start | bytes 6291464 | tf_op jit(solution)/shard_map/ppermute | solution.py:272
  4.0 0.0 copy-start
  4.0 0.0 copy-start.1
  4.0 3.4 %pack.1 = s16[64,72,128]{2,1,0:T(8,128)(2,1)} custom-call(f32[16,128,128]{2,1,0:T(8,128)} %bitcast.17, f32[16,128,128]{2,1,0:T(8,128)} %bitcast.18), custom_call_target="tpu_custom_call" | custom-call | tf_op jit(solution)/shard_map/pack/pallas_call | solution.py:68
  7.4 11.3 %all-to-all-start = ((s16[64,72,128]{2,1,0:T(8,128)(2,1)}), s16[64,72,128]{2,1,0:T(8,128)(2,1)}, u32[]{:S(2)}, u32[]{:S(2)}) async-start(s16[64,72,128]{2,1,0:T(8,128)(2,1)} %pack.1), calls=%async_computation | async-start | bytes 2359296 | tf_op jit(solution)/shard_map/all_to_all | solution.py:282
  18.6 0.0 collective-permute-done.twin_ref
  18.7 0.0 copy-done
  18.7 0.0 copy-done.1
  18.7 2.1 %turn.2.chip_ref = bf16[2048,256]{1,0:T(8,128)(2,1)S(1)} custom-call(s32[1]{0:T(128)} %bitcast.band_ref, s32[2]{0:T(128)S(1)} %copy-done.1, bf16[512,2048]{1,0:T(8,128)(2,1)S(1)} %bitcast.14, bf16[512,2048]{1,0:T(8,128)(2,1)} %collective-permute-done.twin_ref), custom_call_target="tpu_custom_call" | custom-call | tf_op jit(solution)/shard_map/turn/pallas_call | solution.py:120
  20.8 0.0 copy-start.2
  20.8 0.0 copy-start.3
  20.8 2.4 %collective-permute-start.1 = (bf16[2048,256]{1,0:T(8,128)(2,1)S(1)}, bf16[2048,256]{1,0:T(8,128)(2,1)S(1)}, u32[]{:S(2)}, u32[]{:S(2)}) collective-permute-start(bf16[2048,256]{1,0:T(8,128)(2,1)S(1)} %turn.2.chip_ref), channel_id=1, source_target_pairs={{0,130},{1,131},{2,128},{3,129},{4,134},{5,135},{6,132},{7,133},{8... | collective-permute-start | bytes 3145736 | tf_op jit(solution)/shard_map/ppermute | solution.py:274
  23.2 3.2 %turn.3.rest_ref = bf16[2048,256]{1,0:T(8,128)(2,1)} custom-call(s32[1]{0:T(128)} %bitcast.band_ref, s32[2]{0:T(128)} %keepers_ref.5, bf16[512,2048]{1,0:T(8,128)(2,1)} %bitcast.13, bf16[512,2048]{1,0:T(8,128)(2,1)} %collective-permute-done.twin_ref), custom_call_target="tpu_custom_call" | custom-call | tf_op jit(solution)/shard_map/turn/pallas_call | solution.py:120
  26.4 20.6 %collective-permute-done.1.near_ref = bf16[2048,256]{1,0:T(8,128)(2,1)S(1)} collective-permute-done((bf16[2048,256]{1,0:T(8,128)(2,1)S(1)}, bf16[2048,256]{1,0:T(8,128)(2,1)S(1)}, u32[]{:S(2)}, u32[]{:S(2)}) %collective-permute-start.1) | collective-permute-done | bytes 1048608 | tf_op jit(solution)/shard_map/ppermute | solution.py:274
  47.1 0.0 copy-start.4
  47.1 0.6 %collective-permute-start.2 = (bf16[2048,256]{1,0:T(8,128)(2,1)S(1)}, bf16[2048,256]{1,0:T(8,128)(2,1)}, u32[]{:S(2)}, u32[]{:S(2)}) collective-permute-start(bf16[2048,256]{1,0:T(8,128)(2,1)S(1)} %collective-permute-done.1.near_ref), channel_id=1, source_target_pairs={{0,1},{1,0},{2,3},{3,2},{4,5},{5,4},{6,7},{7,6},{8,9},{9,8},{10,11... | collective-permute-start | bytes 3145736 | tf_op jit(solution)/shard_map/ppermute | solution.py:277
  47.7 0.3 all-to-all-done.got_hbm
  48.0 2.1 %collective-permute-done.2.far_ref = bf16[2048,256]{1,0:T(8,128)(2,1)} collective-permute-done((bf16[2048,256]{1,0:T(8,128)(2,1)S(1)}, bf16[2048,256]{1,0:T(8,128)(2,1)}, u32[]{:S(2)}, u32[]{:S(2)}) %collective-permute-start.2) | collective-permute-done | bytes 1048608 | tf_op jit(solution)/shard_map/ppermute | solution.py:277
  50.1 0.0 copy-done.4
  50.1 0.0 copy-done.2
  50.1 0.0 copy-done.3
  50.1 8.5 %rotate.1 = (bf16[2,2048,256]{2,1,0:T(8,128)(2,1)}, bf16[2,2048,256]{2,1,0:T(8,128)(2,1)}) custom-call(s32[1]{0:T(128)} %bitcast.band_ref, s32[2]{0:T(128)S(1)} %copy-done.2, s32[1,256]{1,0:T(1,128)S(1)} %copy-done.3, s16[64,72,128]{2,1,0:T(8,128)(2,1)} %all-to-all-done.got_hbm, bf16[2048,256]{1,0:T(8,128)(2,1)S(1)} %turn.2.chip_ref, ...), custom_call_target="tpu_custom_call" | custom-call | tf_op jit(solution)/shard_map/rotate/pallas_call | solution.py:234
Async XLA Ops:
  0.6 18.0 %collective-permute-start = (bf16[512,2048]{1,0:T(8,128)(2,1)}, bf16[512,2048]{1,0:T(8,128)(2,1)}, u32[]{:S(2)}, u32[]{:S(2)}) collective-permute-start(bf16[512,2048]{1,0:T(8,128)(2,1)} %bitcast.12), channel_id=1, source_target_pairs={{0,1},{1,0},{2,3},{3,2},{4,5},{5,4},{6,7},{7,6},{8,9},{9,8},{10,11... | collective-permute-start | bytes 6291464 | tf_op jit(solution)/shard_map/ppermute | solution.py:272
  4.0 14.7 %copy-start = (bf16[1,512,2048]{2,1,0:T(8,128)(2,1)S(1)}, bf16[1,512,2048]{2,1,0:T(8,128)(2,1)}, u32[]{:S(2)}) copy-start(bf16[1,512,2048]{2,1,0:T(8,128)(2,1)} %param.11) | copy-start | bytes 6291460
  4.0 14.7 %copy-start.1 = (s32[2]{0:T(128)S(1)}, s32[2]{0:T(128)}, u32[]{:S(2)}) copy-start(s32[2]{0:T(128)} %keepers_ref.5) | copy-start | bytes 28
  7.4 40.7 %all-to-all-start = ((s16[64,72,128]{2,1,0:T(8,128)(2,1)}), s16[64,72,128]{2,1,0:T(8,128)(2,1)}, u32[]{:S(2)}, u32[]{:S(2)}) async-start(s16[64,72,128]{2,1,0:T(8,128)(2,1)} %pack.1), calls=%async_computation | async-start | bytes 2359296 | tf_op jit(solution)/shard_map/all_to_all | solution.py:282
  20.8 29.3 %copy-start.2 = (s32[2]{0:T(128)S(1)}, s32[2]{0:T(128)}, u32[]{:S(2)}) copy-start(s32[2]{0:T(128)} %keepers_ref.5) | copy-start | bytes 28
  20.8 29.3 %copy-start.3 = (s32[1,256]{1,0:T(1,128)S(1)}, s32[1,256]{1,0:T(1,128)}, u32[]{:S(2)}) copy-start(s32[1,256]{1,0:T(1,128)} %lat_ref.1) | copy-start | bytes 3076
  20.8 26.2 %collective-permute-start.1 = (bf16[2048,256]{1,0:T(8,128)(2,1)S(1)}, bf16[2048,256]{1,0:T(8,128)(2,1)S(1)}, u32[]{:S(2)}, u32[]{:S(2)}) collective-permute-start(bf16[2048,256]{1,0:T(8,128)(2,1)S(1)} %turn.2.chip_ref), channel_id=1, source_target_pairs={{0,130},{1,131},{2,128},{3,129},{4,134},{5,135},{6,132},{7,133},{8... | collective-permute-start | bytes 3145736 | tf_op jit(solution)/shard_map/ppermute | solution.py:274
  47.1 3.0 %copy-start.4 = (bf16[2048,256]{1,0:T(8,128)(2,1)}, bf16[2048,256]{1,0:T(8,128)(2,1)S(1)}, u32[]{:S(2)}) copy-start(bf16[2048,256]{1,0:T(8,128)(2,1)S(1)} %collective-permute-done.1.near_ref) | copy-start | bytes 3145732
  47.1 3.0 %collective-permute-start.2 = (bf16[2048,256]{1,0:T(8,128)(2,1)S(1)}, bf16[2048,256]{1,0:T(8,128)(2,1)}, u32[]{:S(2)}, u32[]{:S(2)}) collective-permute-start(bf16[2048,256]{1,0:T(8,128)(2,1)S(1)} %collective-permute-done.1.near_ref), channel_id=1, source_target_pairs={{0,1},{1,0},{2,3},{3,2},{4,5},{5,4},{6,7},{7,6},{8,9},{9,8},{10,11... | collective-permute-start | bytes 3145736 | tf_op jit(solution)/shard_map/ppermute | solution.py:277

commit v4 on v3

--- a/solution.py
+++ b/solution.py
@@ -203,12 +203,11 @@
         for s in range(2):
             fetch[2 * t + s].wait()
         rows = slice(starts[t], starts[t] + TILES[t])
-        v = v_ref[rows, :]
+        twice = jnp.concatenate([v_ref[rows, :]] * 2, axis=1)
 
         def product(a, r):
-            return jnp.dot(v, hi_ref[a, r], preferred_element_type=jnp.float32) + jnp.dot(
-                v, lo_ref[a, r], preferred_element_type=jnp.float32
-            )
+            parts = jnp.concatenate([hi_ref[a, r], lo_ref[a, r]], axis=0)
+            return jnp.dot(twice, parts, preferred_element_type=jnp.float32)
 
         for r in range(planes):
             rotated = product(0, r)

time: 58.9 us -> 58.9 us (level)
  no operation moved by 1% of the time
where the time goes in v4:
time: 58.9 us; the launch traced here: 58.6 us
  waiting for transfers between devices  22.6 us (38%)
  starting transfers between devices  18 us (31%)
  Pallas kernels  17.2 us (29%)
  between operations  0.71 us (1%)
    ppermute x1, waiting for transfers between devices, per_device(): near = lax.ppermute(chip, ('pw', 'band'), across)  20.2 us
    all_to_all x1, starting transfers between devices, per_device(): got = lax.all_to_all(sent, 'pw', split_axis=0, concat_axis=0, tiled=True)  11.3 us
    pallas_call x1, Pallas kernels, rotate(): pl.pallas_call(rotate_body, in_specs=[scalar, scalar, near] + [far] * 7,...  8.47 us
    pallas_call x2, Pallas kernels, turn(): pl.pallas_call(functools.partial(turn_body, slot), in_specs=[scalar, scal...  5.34 us
    pallas_call x1, Pallas kernels, pack(): pl.pallas_call(pack_body, in_specs=[anywhere, anywhere], out_specs=anywhe...  3.4 us
    ppermute x1, starting transfers between devices, per_device(): twin = lax.ppermute(own, 'band', swap)  3.33 us
    ppermute x1, starting transfers between devices, per_device(): near = lax.ppermute(chip, ('pw', 'band'), across)  2.4 us
    ppermute x1, waiting for transfers between devices, per_device(): far = lax.ppermute(near, 'band', swap)  2.07 us
  transfers between devices with their start and end apart: 4, of which 3 were waited for; matrix products, arithmetic and copies ran while one was open for 0% of the time, Pallas kernels for 15%

profile of v4, /device:TPU:1, one launch (start us, length us, event | category | flops | bytes accessed | tf_op | source)
XLA Modules:
  0.0 58.6 jit_solution(7808808229558332591)
XLA Ops:
  0.6 3.3 %collective-permute-start = (bf16[512,2048]{1,0:T(8,128)(2,1)}, bf16[512,2048]{1,0:T(8,128)(2,1)}, u32[]{:S(2)}, u32[]{:S(2)}) collective-permute-start(bf16[512,2048]{1,0:T(8,128)(2,1)} %bitcast.12), channel_id=1, source_target_pairs={{0,1},{1,0},{2,3},{3,2},{4,5},{5,4},{6,7},{7,6},{8,9},{9,8},{10,11... | collective-permute-start | bytes 6291464 | tf_op jit(solution)/shard_map/ppermute | solution.py:271
  4.0 0.0 copy-start
  4.0 0.0 copy-start.1
  4.0 3.4 %pack.1 = s16[64,72,128]{2,1,0:T(8,128)(2,1)} custom-call(f32[16,128,128]{2,1,0:T(8,128)} %bitcast.17, f32[16,128,128]{2,1,0:T(8,128)} %bitcast.18), custom_call_target="tpu_custom_call" | custom-call | tf_op jit(solution)/shard_map/pack/pallas_call | solution.py:68
  7.4 11.3 %all-to-all-start = ((s16[64,72,128]{2,1,0:T(8,128)(2,1)}), s16[64,72,128]{2,1,0:T(8,128)(2,1)}, u32[]{:S(2)}, u32[]{:S(2)}) async-start(s16[64,72,128]{2,1,0:T(8,128)(2,1)} %pack.1), calls=%async_computation | async-start | bytes 2359296 | tf_op jit(solution)/shard_map/all_to_all | solution.py:281
  18.6 0.0 collective-permute-done.twin_ref
  18.7 0.0 copy-done
  18.7 0.0 copy-done.1
  18.7 2.1 %turn.2.chip_ref = bf16[2048,256]{1,0:T(8,128)(2,1)S(1)} custom-call(s32[1]{0:T(128)} %bitcast.band_ref, s32[2]{0:T(128)S(1)} %copy-done.1, bf16[512,2048]{1,0:T(8,128)(2,1)S(1)} %bitcast.14, bf16[512,2048]{1,0:T(8,128)(2,1)} %collective-permute-done.twin_ref), custom_call_target="tpu_custom_call" | custom-call | tf_op jit(solution)/shard_map/turn/pallas_call | solution.py:120
  20.8 0.0 copy-start.2
  20.8 0.0 copy-start.3
  20.8 2.4 %collective-permute-start.1 = (bf16[2048,256]{1,0:T(8,128)(2,1)S(1)}, bf16[2048,256]{1,0:T(8,128)(2,1)S(1)}, u32[]{:S(2)}, u32[]{:S(2)}) collective-permute-start(bf16[2048,256]{1,0:T(8,128)(2,1)S(1)} %turn.2.chip_ref), channel_id=1, source_target_pairs={{0,130},{1,131},{2,128},{3,129},{4,134},{5,135},{6,132},{7,133},{8... | collective-permute-start | bytes 3145736 | tf_op jit(solution)/shard_map/ppermute | solution.py:273
  23.2 3.2 %turn.3.rest_ref = bf16[2048,256]{1,0:T(8,128)(2,1)} custom-call(s32[1]{0:T(128)} %bitcast.band_ref, s32[2]{0:T(128)} %keepers_ref.5, bf16[512,2048]{1,0:T(8,128)(2,1)} %bitcast.13, bf16[512,2048]{1,0:T(8,128)(2,1)} %collective-permute-done.twin_ref), custom_call_target="tpu_custom_call" | custom-call | tf_op jit(solution)/shard_map/turn/pallas_call | solution.py:120
  26.4 20.2 %collective-permute-done.1.near_ref = bf16[2048,256]{1,0:T(8,128)(2,1)S(1)} collective-permute-done((bf16[2048,256]{1,0:T(8,128)(2,1)S(1)}, bf16[2048,256]{1,0:T(8,128)(2,1)S(1)}, u32[]{:S(2)}, u32[]{:S(2)}) %collective-permute-start.1) | collective-permute-done | bytes 1048608 | tf_op jit(solution)/shard_map/ppermute | solution.py:273
  46.7 0.0 copy-start.4
  46.7 1.0 %collective-permute-start.2 = (bf16[2048,256]{1,0:T(8,128)(2,1)S(1)}, bf16[2048,256]{1,0:T(8,128)(2,1)}, u32[]{:S(2)}, u32[]{:S(2)}) collective-permute-start(bf16[2048,256]{1,0:T(8,128)(2,1)S(1)} %collective-permute-done.1.near_ref), channel_id=1, source_target_pairs={{0,1},{1,0},{2,3},{3,2},{4,5},{5,4},{6,7},{7,6},{8,9},{9,8},{10,11... | collective-permute-start | bytes 3145736 | tf_op jit(solution)/shard_map/ppermute | solution.py:276
  47.7 0.3 all-to-all-done.got_hbm
  48.0 2.1 %collective-permute-done.2.far_ref = bf16[2048,256]{1,0:T(8,128)(2,1)} collective-permute-done((bf16[2048,256]{1,0:T(8,128)(2,1)S(1)}, bf16[2048,256]{1,0:T(8,128)(2,1)}, u32[]{:S(2)}, u32[]{:S(2)}) %collective-permute-start.2) | collective-permute-done | bytes 1048608 | tf_op jit(solution)/shard_map/ppermute | solution.py:276
  50.1 0.0 copy-done.4
  50.1 0.0 copy-done.2
  50.1 0.0 copy-done.3
  50.1 8.5 %rotate.1 = (bf16[2,2048,256]{2,1,0:T(8,128)(2,1)}, bf16[2,2048,256]{2,1,0:T(8,128)(2,1)}) custom-call(s32[1]{0:T(128)} %bitcast.band_ref, s32[2]{0:T(128)S(1)} %copy-done.2, s32[1,256]{1,0:T(1,128)S(1)} %copy-done.3, s16[64,72,128]{2,1,0:T(8,128)(2,1)} %all-to-all-done.got_hbm, bf16[2048,256]{1,0:T(8,128)(2,1)S(1)} %turn.2.chip_ref, ...), custom_call_target="tpu_custom_call" | custom-call | tf_op jit(solution)/shard_map/rotate/pallas_call | solution.py:233
Async XLA Ops:
  0.6 18.0 %collective-permute-start = (bf16[512,2048]{1,0:T(8,128)(2,1)}, bf16[512,2048]{1,0:T(8,128)(2,1)}, u32[]{:S(2)}, u32[]{:S(2)}) collective-permute-start(bf16[512,2048]{1,0:T(8,128)(2,1)} %bitcast.12), channel_id=1, source_target_pairs={{0,1},{1,0},{2,3},{3,2},{4,5},{5,4},{6,7},{7,6},{8,9},{9,8},{10,11... | collective-permute-start | bytes 6291464 | tf_op jit(solution)/shard_map/ppermute | solution.py:271
  4.0 14.7 %copy-start = (bf16[1,512,2048]{2,1,0:T(8,128)(2,1)S(1)}, bf16[1,512,2048]{2,1,0:T(8,128)(2,1)}, u32[]{:S(2)}) copy-start(bf16[1,512,2048]{2,1,0:T(8,128)(2,1)} %param.11) | copy-start | bytes 6291460
  4.0 14.7 %copy-start.1 = (s32[2]{0:T(128)S(1)}, s32[2]{0:T(128)}, u32[]{:S(2)}) copy-start(s32[2]{0:T(128)} %keepers_ref.5) | copy-start | bytes 28
  7.4 40.7 %all-to-all-start = ((s16[64,72,128]{2,1,0:T(8,128)(2,1)}), s16[64,72,128]{2,1,0:T(8,128)(2,1)}, u32[]{:S(2)}, u32[]{:S(2)}) async-start(s16[64,72,128]{2,1,0:T(8,128)(2,1)} %pack.1), calls=%async_computation | async-start | bytes 2359296 | tf_op jit(solution)/shard_map/all_to_all | solution.py:281
  20.8 29.3 %copy-start.2 = (s32[2]{0:T(128)S(1)}, s32[2]{0:T(128)}, u32[]{:S(2)}) copy-start(s32[2]{0:T(128)} %keepers_ref.5) | copy-start | bytes 28
  20.8 29.3 %copy-start.3 = (s32[1,256]{1,0:T(1,128)S(1)}, s32[1,256]{1,0:T(1,128)}, u32[]{:S(2)}) copy-start(s32[1,256]{1,0:T(1,128)} %lat_ref.1) | copy-start | bytes 3076
  20.8 25.8 %collective-permute-start.1 = (bf16[2048,256]{1,0:T(8,128)(2,1)S(1)}, bf16[2048,256]{1,0:T(8,128)(2,1)S(1)}, u32[]{:S(2)}, u32[]{:S(2)}) collective-permute-start(bf16[2048,256]{1,0:T(8,128)(2,1)S(1)} %turn.2.chip_ref), channel_id=1, source_target_pairs={{0,130},{1,131},{2,128},{3,129},{4,134},{5,135},{6,132},{7,133},{8... | collective-permute-start | bytes 3145736 | tf_op jit(solution)/shard_map/ppermute | solution.py:273
  46.7 3.5 %copy-start.4 = (bf16[2048,256]{1,0:T(8,128)(2,1)}, bf16[2048,256]{1,0:T(8,128)(2,1)S(1)}, u32[]{:S(2)}) copy-start(bf16[2048,256]{1,0:T(8,128)(2,1)S(1)} %collective-permute-done.1.near_ref) | copy-start | bytes 3145732
  46.7 3.4 %collective-permute-start.2 = (bf16[2048,256]{1,0:T(8,128)(2,1)S(1)}, bf16[2048,256]{1,0:T(8,128)(2,1)}, u32[]{:S(2)}, u32[]{:S(2)}) collective-permute-start(bf16[2048,256]{1,0:T(8,128)(2,1)S(1)} %collective-permute-done.1.near_ref), channel_id=1, source_target_pairs={{0,1},{1,0},{2,3},{3,2},{4,5},{5,4},{6,7},{7,6},{8,9},{9,8},{10,11... | collective-permute-start | bytes 3145736 | tf_op jit(solution)/shard_map/ppermute | solution.py:276
